TPU v7x, 512 devices: a whole 4x8x8 slice. The times are simulated.
512 devices in a mesh: blk: 32 (over y_hi, x, core), tp: 16 (over z, y_lo).
Axes of the slice: x: 4, y: 8 (y_hi: 4, y_lo: 2; y = y_hi * 2 + y_lo), z: 8, core: 2. Of those that a mesh axis runs over, the one named last changes fastest.
Arguments:
- tokens: bfloat16 [131072, 896], P(('blk', 'tp')), may hold values from -6 to 6
- cotangent: bfloat16 [131072, 896], P(('blk', 'tp')), may hold values from -0.59765625 to 0.59765625
- weights: bfloat16 [32, 2432, 3, 896], P('blk', 'tp'), may hold values from -6 to 6
- first_moment: bfloat16 [32, 2432, 3, 896], P('blk', 'tp'), may hold values from -0.1796875 to 0.1796875
- second_moment: bfloat16 [32, 2432, 3, 896], P('blk', 'tp'), may hold values from 0.0009994507 to 0.0099487305
Outputs:
- averaged: float32 [32, 2432, 3, 896], P('blk', 'tp')
All inputs are finite; a program needn't handle non-finite values.
Results may differ from a plain program's by a relative error of at most 0.0003.
Values may be sent and summed in bfloat16 or wider, within the bound.
A program may use at most 64 MiB of HBM per device.

v0:
```python
import jax
import jax.numpy as jnp
from jax import lax
from jax.sharding import PartitionSpec as P

STEP = 10


def shifted(block, axis, distance):
    devices = range(lax.axis_size(axis))
    route = [((i - distance) % len(devices), i) for i in devices]
    return lax.ppermute(block, axis, route)


def row_terms(xs, grads_out, rows, hidden_scale):
    width_scale = xs.shape[1] ** (-0.5)
    gate = (
        jnp.einsum("td,nd->tn", xs, rows[:, 0, :], preferred_element_type=jnp.float32) * width_scale
    )
    upper = (
        jnp.einsum("td,nd->tn", xs, rows[:, 1, :], preferred_element_type=jnp.float32) * width_scale
    )
    sigma = jax.nn.sigmoid(gate)
    swish = gate * sigma
    hidden = (swish * upper).astype(jnp.bfloat16)
    back = (
        jnp.einsum("td,nd->tn", grads_out, rows[:, 2, :], preferred_element_type=jnp.float32)
        * hidden_scale
    )
    dgate = (back * upper * sigma * (1.0 + gate * (1.0 - sigma))).astype(jnp.bfloat16)
    dupper = (back * swish).astype(jnp.bfloat16)
    grad_gate = jnp.einsum("tn,td->nd", dgate, xs, preferred_element_type=jnp.float32) * width_scale
    grad_upper = (
        jnp.einsum("tn,td->nd", dupper, xs, preferred_element_type=jnp.float32) * width_scale
    )
    grad_down = (
        jnp.einsum("tn,td->nd", hidden, grads_out, preferred_element_type=jnp.float32)
        * hidden_scale
    )
    return jnp.stack([grad_gate, grad_upper, grad_down], axis=1)


def on_device(tokens, cotangent, weights, first_moment, second_moment):
    own_rows = weights[0]
    local_units = own_rows.shape[0]
    hidden_scale = (local_units * lax.axis_size("tp")) ** (-0.5)
    all_tokens, all_cots = (
        lax.all_gather(tokens, "tp", axis=0, tiled=True),
        lax.all_gather(cotangent, "tp", axis=0, tiled=True),
    )
    grads = row_terms(all_tokens, all_cots, own_rows, hidden_scale)
    moment_one = 0.9 * first_moment[0].astype(jnp.float32) + 0.1 * grads
    moment_two = 0.95 * second_moment[0].astype(jnp.float32) + 0.05 * grads * grads
    correct_one = 1.0 - 0.9**STEP
    correct_two = 1.0 - 0.95**STEP
    master = own_rows.astype(jnp.float32)
    step_size = moment_one / correct_one / (jnp.sqrt(moment_two / correct_two) + 1e-08)
    updated = (master - 0.1 * (step_size + 0.1 * master))[None]
    previous = shifted(updated, "blk", 1)
    following = shifted(updated, "blk", -1)
    return (previous + updated + following) / 3.0


def solution(mesh):
    in_specs = (
        P(("blk", "tp"), None),
        P(("blk", "tp"), None),
        P("blk", "tp", None, None),
        P("blk", "tp", None, None),
        P("blk", "tp", None, None),
    )
    out_specs = P("blk", "tp", None, None)
    return jax.shard_map(
        on_device, mesh=mesh, in_specs=in_specs, out_specs=out_specs, check_vma=False
    )
```

profile of v0, /device:TPU:48, one launch (start us, length us, event | category | flops | bytes accessed | tf_op | source)
XLA Modules:
  0.0 416.1 jit_solution(5356604273082415112)
XLA Ops:
  6.5 0.7 all-gather.5.cloned.1.call-update
  7.3 0.0 all-gather.3.cloned.1.call-start
  7.3 0.7 all-gather.3.cloned.1.call-update
  8.0 171.3 %all-gather.5.cloned.1.call-done = bf16[4096,896]{1,0:T(8,128)(2,1)} async-done(((bf16[256,896]{1,0:T(8,128)(2,1)}), bf16[4096,896]{1,0:T(8,128)(2,1)}) %all-gather.5.cloned.1.call-update) | async-done | bytes 7340048 | tf_op jit(solution)/shard_map/all_gather | solution.py:48
  179.3 6.1 %convolution_multiply_fusion.1 = f32[4096,152]{0,1:T(8,128)S(1)} fusion(bf16[4096,896]{1,0:T(8,128)(2,1)} %all-gather.5.cloned.1.call-done, bf16[152,3,896]{2,0,1:T(8,128)(2,1)} %bitcast.24), kind=kOutput, calls=%fused_computation.1 | convolution fusion | flops 1116307456 | bytes 10102784 | tf_op jit(solution)/shard_map/td,nd->tn/dot_general | solution.py:21
  185.4 0.0 copy-done
  185.4 0.0 copy-done.3
  185.4 4.3 %convolution_multiply_fusion = f32[4096,152]{0,1:T(8,128)} fusion(bf16[4096,896]{1,0:T(8,128)(2,1)S(1)} %copy-done, bf16[152,3,896]{2,0,1:T(8,128)(2,1)S(1)} %bitcast.25), kind=kOutput, calls=%fused_computation | convolution fusion | flops 1116307456 | bytes 10102784 | tf_op jit(solution)/shard_map/td,nd->tn/dot_general | solution.py:18
  189.8 156.4 %all-gather.3.cloned.1.call-done = bf16[4096,896]{1,0:T(8,128)(2,1)} async-done(((bf16[256,896]{1,0:T(8,128)(2,1)}), bf16[4096,896]{1,0:T(8,128)(2,1)}) %all-gather.3.cloned.1.call-update) | async-done | bytes 7340048 | tf_op jit(solution)/shard_map/all_gather | solution.py:49
  346.2 6.1 %convolution_multiply_fusion.2 = f32[4096,152]{0,1:T(8,128)S(1)} fusion(bf16[4096,896]{1,0:T(8,128)(2,1)} %all-gather.3.cloned.1.call-done, bf16[152,3,896]{2,0,1:T(8,128)(2,1)S(1)} %bitcast.26), kind=kOutput, calls=%fused_computation.2 | convolution fusion | flops 1116307456 | bytes 10102784 | tf_op jit(solution)/shard_map/td,nd->tn/dot_general | solution.py:27
  352.3 0.0 slice-start.1
  352.3 1.7 fusion.12
  354.0 0.0 slice-done
  354.0 0.4 slice-done.1
  354.4 1.7 fusion.14
  356.1 0.0 copy-start.4
  356.1 0.0 copy-start.5
  356.1 1.8 fusion.16
  358.0 1.4 convert_subtract_fusion
  359.4 5.3 %collective-permute-start.1 = (f32[1,152,3,896]{3,1,2,0:T(8,128)S(1)}, f32[1,152,3,896]{3,1,2,0:T(8,128)S(1)}, u32[]{:S(2)}, u32[]{:S(2)}) collective-permute-start(f32[1,152,3,896]{3,1,2,0:T(8,128)S(1)} %convert_subtract_fusion), channel_id=1, source_target_pairs={{16,0},{32,16},{48,32},{64,48},{80,64},{96,80},{112,96},{128,112},... | collective-permute-start | bytes 4902920 | tf_op jit(solution)/shard_map/ppermute | solution.py:12
  364.7 1.9 collective-permute-start
  366.6 33.9 %collective-permute-done.1 = f32[1,152,3,896]{3,1,2,0:T(8,128)S(1)} collective-permute-done((f32[1,152,3,896]{3,1,2,0:T(8,128)S(1)}, f32[1,152,3,896]{3,1,2,0:T(8,128)S(1)}, u32[]{:S(2)}, u32[]{:S(2)}) %collective-permute-start.1) | collective-permute-done | bytes 1634336 | tf_op jit(solution)/shard_map/ppermute | solution.py:12
  400.5 7.2 %collective-permute-done = f32[1,152,3,896]{3,1,2,0:T(8,128)S(1)} collective-permute-done((f32[1,152,3,896]{3,1,2,0:T(8,128)S(1)}, f32[1,152,3,896]{3,1,2,0:T(8,128)S(1)}, u32[]{:S(2)}, u32[]{:S(2)}) %collective-permute-start) | collective-permute-done | bytes 1634336 | tf_op jit(solution)/shard_map/ppermute | solution.py:12
  407.7 1.5 add_multiply_fusion
  (11 shorter events, 0.0 us)
Async XLA Ops:
  6.5 172.8 %all-gather.5.cloned.1.call-start = ((), (), s32[]{:S(2)}) async-start(), calls=%async_computation.1 | async-start | bytes 7798784 | tf_op jit(solution)/shard_map/all_gather | solution.py:48
  7.3 338.9 %all-gather.3.cloned.1.call-start = ((), (), s32[]{:S(2)}) async-start(), calls=%async_computation | async-start | bytes 7798784 | tf_op jit(solution)/shard_map/all_gather | solution.py:49
  179.3 6.1 %copy-start = (bf16[4096,896]{1,0:T(8,128)(2,1)S(1)}, bf16[4096,896]{1,0:T(8,128)(2,1)}, u32[]{:S(2)}) copy-start(bf16[4096,896]{1,0:T(8,128)(2,1)} %all-gather.5.cloned.1.call-done) | copy-start | bytes 22020100
  179.3 6.1 %copy-start.3 = (bf16[1,152,3,896]{3,1,2,0:T(8,128)(2,1)S(1)}, bf16[1,152,3,896]{3,1,2,0:T(8,128)(2,1)}, u32[]{:S(2)}) copy-start(bf16[1,152,3,896]{3,1,2,0:T(8,128)(2,1)} %param.7) | copy-start | bytes 2451460
  346.2 6.1 %copy-start.1 = (bf16[4096,896]{1,0:T(8,128)(2,1)S(1)}, bf16[4096,896]{1,0:T(8,128)(2,1)}, u32[]{:S(2)}) copy-start(bf16[4096,896]{1,0:T(8,128)(2,1)} %all-gather.3.cloned.1.call-done) | copy-start | bytes 22020100
  346.2 6.1 %copy-start.2 = (f32[4096,152]{0,1:T(8,128)S(1)}, f32[4096,152]{0,1:T(8,128)}, u32[]{:S(2)}) copy-start(f32[4096,152]{0,1:T(8,128)} %convolution_multiply_fusion) | copy-start | bytes 7471108
  346.2 7.8 %slice-start = ((s8[7340032]{0:T(1024)(128)(4,1)}), s8[4194304]{0:T(1024)(128)(4,1)S(1)}, s32[]{:S(2)}) async-start(s8[7340032]{0:T(1024)(128)(4,1)} %bitcast.22), calls=%async_computation.2 | async-start | bytes 8388608
  352.3 2.1 slice-start.1
  356.1 1.9 copy-start.4
  356.1 1.9 copy-start.5
  359.4 41.1 %collective-permute-start.1 = (f32[1,152,3,896]{3,1,2,0:T(8,128)S(1)}, f32[1,152,3,896]{3,1,2,0:T(8,128)S(1)}, u32[]{:S(2)}, u32[]{:S(2)}) collective-permute-start(f32[1,152,3,896]{3,1,2,0:T(8,128)S(1)} %convert_subtract_fusion), channel_id=1, source_target_pairs={{16,0},{32,16},{48,32},{64,48},{80,64},{96,80},{112,96},{128,112},... | collective-permute-start | bytes 4902920 | tf_op jit(solution)/shard_map/ppermute | solution.py:12
  364.7 43.0 %collective-permute-start = (f32[1,152,3,896]{3,1,2,0:T(8,128)S(1)}, f32[1,152,3,896]{3,1,2,0:T(8,128)S(1)}, u32[]{:S(2)}, u32[]{:S(2)}) collective-permute-start(f32[1,152,3,896]{3,1,2,0:T(8,128)S(1)} %convert_subtract_fusion), channel_id=1, source_target_pairs={{496,0},{0,16},{16,32},{32,48},{48,64},{64,80},{80,96},{96,112},{1... | collective-permute-start | bytes 4902920 | tf_op jit(solution)/shard_map/ppermute | solution.py:12
Sparse Core Ops, SparseCore 0:
  9.4 169.8 all-gather.4
  181.4 164.7 all-gather.2
where the time goes:
time: 416 us
  waiting for transfers between devices  370 us (89%)
  matrix products  21.7 us (5%)
  between operations  13.5 us (3%)
  starting transfers between devices  7.25 us (2%)
    all_gather x1, waiting for transfers between devices, on_device(): lax.all_gather(tokens, 'tp', axis=0, tiled=True)  171 us
    all_gather x1, waiting for transfers between devices, on_device(): lax.all_gather(cotangent, 'tp', axis=0, tiled=True)  156 us
    ppermute x2, waiting for transfers between devices, shifted(): return lax.ppermute(block, axis, route)  41.1 us
  transfers between devices with their start and end apart: 4, of which 4 were waited for; matrix products, arithmetic and copies ran while one was open for 3% of the time, Pallas kernels for 0%

commit v1 on v0

--- a/solution.py
+++ b/solution.py
@@ -45,7 +45,9 @@
     local_units = own_rows.shape[0]
     hidden_scale = (local_units * lax.axis_size("tp")) ** (-0.5)
     all_tokens, all_cots = (
-        lax.all_gather(tokens, "tp", axis=0, tiled=True),
+        jnp.concatenate(
+            lax.all_to_all(jnp.stack([tokens] * lax.axis_size("tp")), "tp", 0, 0), axis=0
+        ),
         lax.all_gather(cotangent, "tp", axis=0, tiled=True),
     )
     grads = row_terms(all_tokens, all_cots, own_rows, hidden_scale)

time: 416 us -> 368 us (0.88)
  the two profiles are of different devices: /device:TPU:48 before, /device:TPU:72 now
where the time goes in v1:
time: 368 us
  waiting for transfers between devices  295 us (80%)
  matrix products  31 us (8%)
  starting transfers between devices  20.9 us (6%)
  between operations  13.5 us (4%)
  local copies, waits for them, and re-layouts  5 us (1%)
    all_to_all x1, waiting for transfers between devices, on_device(): lax.all_to_all(jnp.stack([tokens] * lax.axis_size('tp')), 'tp', 0, 0)  205 us
    all_gather x1, waiting for transfers between devices, on_device(): lax.all_gather(cotangent, 'tp', axis=0, tiled=True)  47.5 us
    ppermute x2, waiting for transfers between devices, shifted(): return lax.ppermute(block, axis, route)  40.9 us
    all_to_all x1, starting transfers between devices, on_device(): lax.all_to_all(jnp.stack([tokens] * lax.axis_size('tp')), 'tp', 0, 0)  11 us
    ppermute x2, starting transfers between devices, shifted(): return lax.ppermute(block, axis, route)  9.82 us
    dot_general x1, matrix products, row_terms(): jnp.einsum('td,nd->tn', xs, rows[:, 0, :], preferred_element_type=jnp.flo...  7.38 us
  transfers between devices with their start and end apart: 4, of which 4 were waited for; matrix products, arithmetic and copies ran while one was open for 4% of the time, Pallas kernels for 0%

profile of v1, /device:TPU:72, one launch (start us, length us, event | category | flops | bytes accessed | tf_op | source)
XLA Modules:
  0.0 367.9 jit_solution(7087371173608720490)
XLA Ops:
  6.5 5.0 %stack.10 = bf16[16,256,896]{2,1,0:T(8,128)(2,1)} broadcast(bf16[256,896]{1,0:T(8,128)(2,1)} %param.5), dimensions={1,2} | broadcast | bytes 7798784 | tf_op jit(solution)/shard_map/stack | solution.py:49
  11.5 11.0 %all-to-all-start = ((bf16[16,256,896]{2,1,0:T(8,128)(2,1)}), bf16[16,256,896]{2,1,0:T(8,128)(2,1)}, u32[]{:S(2)}, u32[]{:S(2)}) async-start(bf16[16,256,896]{2,1,0:T(8,128)(2,1)} %stack.10), calls=%async_computation | async-start | bytes 14680064 | tf_op jit(solution)/shard_map/all_to_all | solution.py:49
  22.5 0.0 all-gather.2.cloned.1.call-start
  22.6 0.7 all-gather.2.cloned.1.call-update
  23.3 205.5 %all-to-all-done = bf16[16,256,896]{2,1,0:T(8,128)(2,1)} async-done(((bf16[16,256,896]{2,1,0:T(8,128)(2,1)}), bf16[16,256,896]{2,1,0:T(8,128)(2,1)}, u32[]{:S(2)}, u32[]{:S(2)}) %all-to-all-start) | async-done | bytes 7340064 | tf_op jit(solution)/shard_map/all_to_all | solution.py:49
  228.7 6.0 %convolution_multiply_fusion.1 = f32[4096,152]{0,1:T(8,128)S(1)} fusion(bf16[4096,896]{1,0:T(8,128)(2,1)} %bitcast.2, bf16[152,3,896]{2,0,1:T(8,128)(2,1)S(1)} %bitcast.25), kind=kOutput, calls=%fused_computation.1 | convolution fusion | flops 1116307456 | bytes 10102784 | tf_op jit(solution)/shard_map/td,nd->tn/dot_general | solution.py:21
  234.7 7.4 %convolution_multiply_fusion = f32[4096,152]{0,1:T(8,128)} fusion(bf16[4096,896]{1,0:T(8,128)(2,1)} %bitcast.2, bf16[152,3,896]{2,0,1:T(8,128)(2,1)S(1)} %bitcast.26), kind=kOutput, calls=%fused_computation | convolution fusion | flops 1116307456 | bytes 10102784 | tf_op jit(solution)/shard_map/td,nd->tn/dot_general | solution.py:18
  242.1 47.5 %all-gather.2.cloned.1.call-done = bf16[4096,896]{1,0:T(8,128)(2,1)} async-done(((bf16[256,896]{1,0:T(8,128)(2,1)}), bf16[4096,896]{1,0:T(8,128)(2,1)}) %all-gather.2.cloned.1.call-update) | async-done | bytes 7340048 | tf_op jit(solution)/shard_map/all_gather | solution.py:51
  289.5 6.1 %convolution_multiply_fusion.2 = f32[4096,152]{0,1:T(8,128)S(1)} fusion(bf16[4096,896]{1,0:T(8,128)(2,1)} %all-gather.2.cloned.1.call-done, bf16[152,3,896]{2,0,1:T(8,128)(2,1)S(1)} %bitcast.27), kind=kOutput, calls=%fused_computation.2 | convolution fusion | flops 1116307456 | bytes 10102784 | tf_op jit(solution)/shard_map/td,nd->tn/dot_general | solution.py:27
  295.6 0.0 slice-start
  295.6 4.9 %fusion.14 = f32[1,152,1,896]{3,1,2,0:T(8,128)S(1)} fusion(bf16[4096,896]{1,0:T(8,128)(2,1)} %bitcast.2, f32[4096,152]{0,1:T(8,128)S(1)} %convolution_multiply_fusion.2, f32[4096,152]{0,1:T(8,128)S(1)} %copy-done), kind=kOutput, calls=%fused_computation.26 | convolution fusion | flops 1119556608 | bytes 12865536 | tf_op jit(solution)/shard_map/tn,td->nd/dot_general | solution.py:34
  300.5 0.0 slice-start.1
  300.5 5.1 %fusion.16 = f32[1,152,1,896]{3,1,2,0:T(8,128)S(1)} fusion(bf16[4096,896]{1,0:T(8,128)(2,1)} %bitcast.2, f32[4096,152]{0,1:T(8,128)S(1)} %copy-done, f32[4096,152]{0,1:T(8,128)S(1)} %convolution_multiply_fusion.2, f32[4096,152]{0,1:T(8,128)S(1)} %convolution_multiply_fusion.1), kind=kOutput, calls=%fused_computation.28 | convolution fusion | flops 1122046976 | bytes 15355904 | tf_op jit(solution)/shard_map/tn,td->nd/dot_general | solution.py:32
  305.6 0.0 copy-start.2
  305.6 0.0 copy-start.3
  305.7 1.7 fusion.12
  307.3 0.0 copy-done.2
  307.3 0.0 copy-done.3
  307.4 1.4 convert_subtract_fusion
  308.8 7.9 %collective-permute-start.1 = (f32[1,152,3,896]{3,1,2,0:T(8,128)S(1)}, f32[1,152,3,896]{3,1,2,0:T(8,128)S(1)}, u32[]{:S(2)}, u32[]{:S(2)}) collective-permute-start(f32[1,152,3,896]{3,1,2,0:T(8,128)S(1)} %convert_subtract_fusion), channel_id=1, source_target_pairs={{16,0},{32,16},{48,32},{64,48},{80,64},{96,80},{112,96},{128,112},... | collective-permute-start | bytes 4902920 | tf_op jit(solution)/shard_map/ppermute | solution.py:12
  316.7 1.9 collective-permute-start
  318.6 32.9 %collective-permute-done.1 = f32[1,152,3,896]{3,1,2,0:T(8,128)S(1)} collective-permute-done((f32[1,152,3,896]{3,1,2,0:T(8,128)S(1)}, f32[1,152,3,896]{3,1,2,0:T(8,128)S(1)}, u32[]{:S(2)}, u32[]{:S(2)}) %collective-permute-start.1) | collective-permute-done | bytes 1634336 | tf_op jit(solution)/shard_map/ppermute | solution.py:12
  351.5 8.0 %collective-permute-done = f32[1,152,3,896]{3,1,2,0:T(8,128)S(1)} collective-permute-done((f32[1,152,3,896]{3,1,2,0:T(8,128)S(1)}, f32[1,152,3,896]{3,1,2,0:T(8,128)S(1)}, u32[]{:S(2)}, u32[]{:S(2)}) %collective-permute-start) | collective-permute-done | bytes 1634336 | tf_op jit(solution)/shard_map/ppermute | solution.py:12
  359.5 1.5 add_multiply_fusion
  (7 shorter events, 0.0 us)
Async XLA Ops:
  11.5 217.2 %copy-start.1 = (bf16[1,152,3,896]{3,1,2,0:T(8,128)(2,1)S(1)}, bf16[1,152,3,896]{3,1,2,0:T(8,128)(2,1)}, u32[]{:S(2)}) copy-start(bf16[1,152,3,896]{3,1,2,0:T(8,128)(2,1)} %param.7) | copy-start | bytes 2451460
  11.5 217.2 %all-to-all-start = ((bf16[16,256,896]{2,1,0:T(8,128)(2,1)}), bf16[16,256,896]{2,1,0:T(8,128)(2,1)}, u32[]{:S(2)}, u32[]{:S(2)}) async-start(bf16[16,256,896]{2,1,0:T(8,128)(2,1)} %stack.10), calls=%async_computation | async-start | bytes 14680064 | tf_op jit(solution)/shard_map/all_to_all | solution.py:49
  22.5 267.0 %all-gather.2.cloned.1.call-start = ((), (), s32[]{:S(2)}) async-start(), calls=%async_computation.1 | async-start | bytes 7798784 | tf_op jit(solution)/shard_map/all_gather | solution.py:51
  289.5 6.1 %copy-start = (f32[4096,152]{0,1:T(8,128)S(1)}, f32[4096,152]{0,1:T(8,128)}, u32[]{:S(2)}) copy-start(f32[4096,152]{0,1:T(8,128)} %convolution_multiply_fusion) | copy-start | bytes 7471108
  295.6 10.0 %slice-start = ((s8[7340032]{0:T(1024)(128)(4,1)}), s8[4194304]{0:T(1024)(128)(4,1)S(1)}, s32[]{:S(2)}) async-start(s8[7340032]{0:T(1024)(128)(4,1)} %bitcast.23), calls=%async_computation.2 | async-start | bytes 8388608
  300.5 5.1 %slice-start.1 = ((s8[7340032]{0:T(1024)(128)(4,1)}), s8[3145728]{0:T(1024)(128)(4,1)S(1)}, s32[]{:S(2)}) async-start(s8[7340032]{0:T(1024)(128)(4,1)} %bitcast.23), calls=%async_computation.3 | async-start | bytes 6291456
  305.6 1.7 copy-start.2
  305.6 1.7 copy-start.3
  308.8 42.7 %collective-permute-start.1 = (f32[1,152,3,896]{3,1,2,0:T(8,128)S(1)}, f32[1,152,3,896]{3,1,2,0:T(8,128)S(1)}, u32[]{:S(2)}, u32[]{:S(2)}) collective-permute-start(f32[1,152,3,896]{3,1,2,0:T(8,128)S(1)} %convert_subtract_fusion), channel_id=1, source_target_pairs={{16,0},{32,16},{48,32},{64,48},{80,64},{96,80},{112,96},{128,112},... | collective-permute-start | bytes 4902920 | tf_op jit(solution)/shard_map/ppermute | solution.py:12
  316.7 42.9 %collective-permute-start = (f32[1,152,3,896]{3,1,2,0:T(8,128)S(1)}, f32[1,152,3,896]{3,1,2,0:T(8,128)S(1)}, u32[]{:S(2)}, u32[]{:S(2)}) collective-permute-start(f32[1,152,3,896]{3,1,2,0:T(8,128)S(1)} %convert_subtract_fusion), channel_id=1, source_target_pairs={{496,0},{0,16},{16,32},{32,48},{48,64},{64,80},{80,96},{96,112},{1... | collective-permute-start | bytes 4902920 | tf_op jit(solution)/shard_map/ppermute | solution.py:12
Sparse Core Ops, SparseCore 0:
  25.4 264.0 all-gather.1
